TPU v7x, 256 devices: a whole 4x4x8 slice. The times are simulated.
256 devices in a mesh: gx: 8 (over x, core), gy: 4 (over y), gz: 8 (over z).
Axes of the slice: x: 4, y: 4, z: 8, core: 2. Of those that a mesh axis runs over, the one named last changes fastest.
Arguments:
- t_matrix: float32 [1, 8, 4, 32, 1024], P(None, 'gx', 'gy', 'gz'), may hold values from -3 to 3
- structure: float32 [1, 1440, 1440], replicated, may hold values from -0.0390625 to 0.0390625
- species: int32 [8, 4, 32], P('gx', 'gy', 'gz'), may hold values from 0 to 3
- members: int32 [8, 4, 32, 45], P('gx', 'gy', 'gz'), may hold values from -1 to 44, as said below
- delta_table: float32 [4, 1024], replicated, may hold values from -4 to 4
Outputs:
- site_tau: float32 [1, 8, 4, 32, 1024], P(None, 'gx', 'gy', 'gz')
- pair_terms: float32 [8, 4, 32, 45], P('gx', 'gy', 'gz')
Inputs may be any that keep to these rules, and one draw needn't show every extreme that they name: `members`: each site's list names distinct window cells, the centre cell first, 27 to 45 of them, then -1 in the remaining slots; in every draw some site lists all 45 cells.
All inputs are finite; a program needn't handle non-finite values.
Results may differ from a plain program's by a relative error of at most 0.00013.
Values sent between devices are 32-bit elements; how exact they have to be, the bound alone decides.
A program may use at most 192 MiB of HBM per device.

v0:
```python
import jax
import jax.numpy as jnp
from jax import lax
from jax.experimental import pallas as pl
from jax.experimental.pallas import tpu as pltpu
from jax.sharding import PartitionSpec as P

L2 = 32
WINDOW = 45
ITERS = 4
SPECIES = 4
DEPTH = 4
LANES = DEPTH * L2
ROWS = WINDOW * L2
PADDED = 1536
CHUNK = ROWS // 3
CELLS = WINDOW // 3
CENTRE = WINDOW // 2
F32 = jnp.float32
BF16 = jnp.bfloat16
MESH = pl.DeviceIdType.MESH


def split(x):
    high = x.astype(BF16)
    return high, (x - high.astype(F32)).astype(BF16)


def dot(a, b):
    return jnp.dot(a, b, preferred_element_type=F32)


def kernel(
    t_ref,
    s_hbm,
    species_ref,
    members_ref,
    dtab_ref,
    tau_ref,
    pair_ref,
    sf,
    sh,
    sl,
    w,
    tw,
    halo_c,
    halo_l,
    halo_r,
    pack_u,
    pack_d,
    mask,
    blocks,
    dbd,
    rnat,
    rb,
    prow,
    msend,
    usend,
    dsend,
    mrecv,
    urecv,
    drecv,
    s_sem,
    hc_send,
    hl_send,
    hr_send,
    hc_recv,
    hl_recv,
    hr_recv,
    m_send,
    u_send,
    d_send,
    m_recv,
    u_recv,
    d_recv,
):
    gx, gy, gz = lax.axis_index("gx"), lax.axis_index("gy"), lax.axis_index("gz")
    nx, ny, nz = lax.axis_size("gx"), lax.axis_size("gy"), lax.axis_size("gz")

    def peer(dx, dy, dz):
        return (
            lax.rem(gx + dx + nx, nx),
            lax.rem(gy + dy + ny, ny),
            lax.rem(gz + dz + nz, nz),
        )

    def rows_copy(i):
        rows = pl.ds(pl.multiple_of(i * 160, 160), 160)
        return pltpu.make_async_copy(s_hbm.at[0, rows, :], sf.at[rows, :], s_sem.at[i])

    @pl.loop(0, 9)
    def _(i):
        rows_copy(i).start()

    barrier = pltpu.get_barrier_semaphore()

    @pl.loop(0, 27)
    def _(n):
        @pl.when(n != 13)
        def _():
            pl.semaphore_signal(
                barrier,
                inc=1,
                device_id=peer(n // 9 - 1, lax.rem(n // 3, 3) - 1, lax.rem(n, 3) - 1),
                device_id_type=MESH,
            )

    lane = lax.broadcasted_iota(jnp.int32, (L2, LANES), 1)
    lane16 = lax.broadcasted_iota(jnp.int32, (L2 // 2, LANES), 1)
    t = t_ref[...]
    top, low = t[: L2 // 2], t[L2 // 2 :]
    pack_u[...] = jnp.where(lane16 < 64, pltpu.roll(top, 64, 1), low)
    pack_d[...] = jnp.where(lane16 < 64, top, pltpu.roll(low, 64, 1))
    halo_c[4] = t

    pl.semaphore_wait(barrier, 26)

    def remote(src, dst, send, recv, device):
        return pltpu.make_async_remote_copy(
            src_ref=src,
            dst_ref=dst,
            send_sem=send,
            recv_sem=recv,
            device_id=device,
            device_id_type=MESH,
        )

    def halo(plane):
        dx, dy = plane // 3 - 1, lax.rem(plane, 3) - 1
        slot = 8 - plane
        c = remote(t_ref, halo_c.at[slot], hc_send.at[plane], hc_recv.at[slot], peer(dx, dy, 0))
        u = remote(pack_u, halo_l.at[slot], hl_send.at[plane], hl_recv.at[slot], peer(dx, dy, 1))
        d = remote(pack_d, halo_r.at[slot], hr_send.at[plane], hr_recv.at[slot], peer(dx, dy, -1))
        return c, u, d

    @pl.loop(0, 9)
    def _(plane):
        c, u, d = halo(plane)

        @pl.when(plane != 4)
        def _():
            c.start()

        u.start()
        d.start()

    cells = lax.broadcasted_iota(jnp.int32, (48, WINDOW), 0)
    lane48 = lax.broadcasted_iota(jnp.int32, (48, LANES), 1)
    member = jnp.zeros((48, LANES), F32)
    for s in range(DEPTH):
        hit = jnp.where(members_ref[s : s + 1, :] == cells, 1.0, 0.0).astype(F32)
        some = jnp.max(hit, axis=1, keepdims=True)
        member = jnp.where(lane48 // L2 == s, some, member)
    mask[...] = member

    br = lax.broadcasted_iota(jnp.int32, (LANES, LANES), 0)
    bc = lax.broadcasted_iota(jnp.int32, (LANES, LANES), 1)
    blocks[...] = jnp.where(br // L2 == bc // L2, 1.0, 0.0).astype(BF16)

    for s in range(DEPTH):
        own = dtab_ref[0]
        for k in range(1, SPECIES):
            own = jnp.where(species_ref[s] == k, dtab_ref[k], own)
        dh, dl = split(jnp.where(lane // L2 == s, own, 0.0))
        rows = slice(s * L2, (s + 1) * L2)
        down = slice(LANES + s * L2, LANES + (s + 1) * L2)
        dbd[rows, :LANES] = dh
        dbd[rows, LANES:] = dl
        dbd[down, :LANES] = dh
        dbd[down, LANES:] = jnp.zeros((L2, LANES), BF16)

    w[:, 512:768, :] = jnp.zeros((2, 256, 2 * LANES), BF16)
    w[:, ROWS:, :] = jnp.zeros((2, PADDED - ROWS, 2 * LANES), BF16)
    th, tl = split(t)
    w[0, CENTRE * L2 : (CENTRE + 1) * L2, :LANES] = th
    w[0, CENTRE * L2 : (CENTRE + 1) * L2, LANES:] = tl
    sh[:, ROWS:] = jnp.zeros((ROWS, PADDED - ROWS), BF16)
    sl[:, ROWS:] = jnp.zeros((ROWS, PADDED - ROWS), BF16)

    @pl.loop(0, 9)
    def _(i):
        rows_copy(i).wait()
        rows = pl.ds(pl.multiple_of(i * 160, 160), 160)
        high, rest = split(sf[rows, :])
        sh[rows, :ROWS] = high
        sl[rows, :ROWS] = rest

    @pl.loop(0, 9)
    def _(plane):
        c, u, d = halo(8 - plane)

        @pl.when(plane != 4)
        def _():
            c.wait_recv()

        u.wait_recv()
        d.wait_recv()
        centre = halo_c[plane]
        up, down = halo_l[plane], halo_r[plane]
        left = jnp.concatenate([pltpu.roll(up, 64, 1), up], axis=0)
        right = jnp.concatenate([down, pltpu.roll(down, 64, 1)], axis=0)
        windows = [
            pltpu.roll(jnp.where(lane < 64, centre, left), 64, 1),
            pltpu.roll(jnp.where(lane < 96, centre, left), 32, 1),
            centre,
            pltpu.roll(jnp.where(lane < 32, right, centre), 96, 1),
            pltpu.roll(jnp.where(lane < 64, right, centre), 64, 1),
        ]
        for k in range(5):
            cell = plane * 5 + k
            th, tl = split(windows[k] * mask[pl.ds(cell, 1), :])
            tw[cell, :L2] = th
            tw[cell, L2:] = tl

    def chunk(g, now, later, first=False, last=False):
        rows = pl.ds(pl.multiple_of(g * CHUNK, CHUNK), CHUNK)
        if first:
            wide = w[0, 512:768, :]
            a = dot(sh[rows, 512:768], wide)
            b = dot(sl[rows, 512:768], wide[:, :LANES])
        else:
            wide = w[now]
            a = dot(sh[rows, :], wide)
            b = dot(sl[rows, :], wide[:, :LANES])
        image = a[:, :LANES] + (a[:, LANES:] + b)
        on = blocks[...]
        columns = []
        for i in range(CELLS):
            ih, il = split(image[i * L2 : (i + 1) * L2])
            wbd = jnp.concatenate(
                [
                    jnp.concatenate([ih] * DEPTH, axis=0) * on,
                    jnp.concatenate([il] * DEPTH, axis=0) * on,
                ],
                axis=1,
            )
            res = dot(tw[g * CELLS + i], wbd)
            x = res[:L2, :LANES] + (res[:L2, LANES:] + res[L2:, :LANES])
            if i == CELLS // 2:
                x = x + t_ref[...] * jnp.where(g == 1, 1.0, 0.0).astype(F32)
                if last:

                    @pl.when(g == 1)
                    def _():
                        tau_ref[...] = x

            xh, xl = split(x)
            columns.append(jnp.concatenate([xh, xl], axis=1))
        columns = jnp.concatenate(columns, axis=0)
        if not last:
            w[later, rows, :] = columns
            return
        r2 = dot(columns, dbd[...])
        r = r2[:, :LANES] + r2[:, LANES:]
        rnat[rows, :] = r
        for j in range(3):
            turned = []
            for k in range(5):
                at = (j * 5 + k) * L2
                block = r[at : at + L2]
                turned.append(pltpu.roll(block, (L2 * (k - 2)) % LANES, 1) if k != 2 else block)
            plane = g * 3 + j
            kept = [
                turned[2],
                turned[3],
                turned[1],
                jnp.where(lane >= 64, turned[4], turned[0]),
            ]
            usend[plane] = jnp.where(lane < 64, turned[4], pltpu.roll(turned[3], 64, 1))
            dsend[plane] = jnp.where(lane >= 64, turned[0], pltpu.roll(turned[1], 64, 1))
            c, u, d = pairs(plane)
            u.start()
            d.start()

            def away():
                for n in range(4):
                    msend[plane, n] = kept[n]
                c.start()

            if j == 1:
                pl.when(g != 1)(away)

                @pl.when(g == 1)
                def _():
                    for n in range(4):
                        mrecv[4, n] = kept[n]
            else:
                away()

    def pairs(plane):
        dx, dy = plane // 3 - 1, lax.rem(plane, 3) - 1
        c = remote(msend.at[plane], mrecv.at[plane], m_send.at[plane], m_recv.at[plane], peer(dx, dy, 0))
        u = remote(usend.at[plane], urecv.at[plane], u_send.at[plane], u_recv.at[plane], peer(dx, dy, 1))
        d = remote(dsend.at[plane], drecv.at[plane], d_send.at[plane], d_recv.at[plane], peer(dx, dy, -1))
        return c, u, d

    @pl.loop(0, 3)
    def _(g):
        chunk(g, 0, 1, first=True)

    @pl.loop(0, (ITERS - 2) * 3)
    def _(n):
        now = lax.rem(n // 3 + 1, 2)
        chunk(lax.rem(n, 3), now, 1 - now)

    @pl.loop(0, 3)
    def _(n):
        chunk(lax.rem(2 * n, 3), (ITERS - 1) % 2, 0, last=True)

    rnat[ROWS:, :] = jnp.zeros((PADDED - ROWS, LANES), F32)

    @pl.loop(0, 12)
    def _(i):
        turned = rnat[pl.ds(pl.multiple_of(i * LANES, LANES), LANES), :].T
        for j in range(4):
            out = None
            for s in range(DEPTH):
                part = turned[s * L2 : (s + 1) * L2]
                shift = (L2 * (s - j)) % LANES
                part = pltpu.roll(part, shift, 1) if shift else part
                out = part if out is None else jnp.where(lane // L2 == s, part, out)
            rb[i * 4 + j] = out

    @pl.loop(0, 9)
    def _(n):
        plane = jnp.where(n == 0, 4, jnp.where(n <= 4, n - 1, n))
        c, u, d = pairs(plane)

        @pl.when(n != 0)
        def _():
            c.wait_recv()

        u.wait_recv()
        d.wait_recv()
        up, down = urecv[plane], drecv[plane]
        split_block = mrecv[plane, 3]
        got = [
            jnp.where(lane < 64, split_block, down),
            jnp.where(lane < 96, mrecv[plane, 2], pltpu.roll(down, 64, 1)),
            mrecv[plane, 0],
            jnp.where(lane < 32, pltpu.roll(up, 64, 1), mrecv[plane, 1]),
            jnp.where(lane < 64, up, split_block),
        ]
        for k in range(5):
            cell = WINDOW - 1 - (plane * 5 + k)
            prow[pl.ds(cell, 1), :] = jnp.sum(got[k] * rb[cell], axis=0, keepdims=True)

    prow[WINDOW:, :] = jnp.zeros((48 - WINDOW, LANES), F32)
    sr = lax.broadcasted_iota(jnp.int32, (8, LANES), 0)
    sc = lax.broadcasted_iota(jnp.int32, (8, LANES), 1)
    chosen = jnp.where(sc // L2 == sr, 1.0, 0.0).astype(F32)
    sums = lax.dot_general(
        chosen,
        prow[...],
        (((1,), (1,)), ((), ())),
        precision=lax.Precision.HIGHEST,
        preferred_element_type=F32,
    )
    pair_ref[...] = sums[:DEPTH, :WINDOW]

    @pl.loop(0, 9)
    def _(plane):
        for copies in (halo(plane), pairs(plane)):
            c, u, d = copies

            @pl.when(plane != 4)
            def _():
                c.wait_send()

            u.wait_send()
            d.wait_send()


def body(t_matrix, structure, species, members, delta_table):
    t = t_matrix.reshape(DEPTH, L2, L2).transpose(1, 0, 2).reshape(L2, LANES)
    dtab = jnp.tile(delta_table.reshape(SPECIES, L2, L2), (1, 1, DEPTH))
    vmem = pl.BlockSpec(memory_space=pltpu.VMEM)
    dma = pltpu.SemaphoreType.DMA
    tau, pair = pl.pallas_call(
        kernel,
        out_shape=(
            jax.ShapeDtypeStruct((L2, LANES), F32),
            jax.ShapeDtypeStruct((DEPTH, WINDOW), F32),
        ),
        in_specs=[
            vmem,
            pl.BlockSpec(memory_space=pl.ANY),
            pl.BlockSpec(memory_space=pltpu.SMEM),
            vmem,
            vmem,
        ],
        out_specs=(vmem, vmem),
        scratch_shapes=[
            pltpu.VMEM((ROWS, ROWS), F32),
            pltpu.VMEM((ROWS, PADDED), BF16),
            pltpu.VMEM((ROWS, PADDED), BF16),
            pltpu.VMEM((2, PADDED, 2 * LANES), BF16),
            pltpu.VMEM((WINDOW, 2 * L2, LANES), BF16),
            pltpu.VMEM((9, L2, LANES), F32),
            pltpu.VMEM((9, L2 // 2, LANES), F32),
            pltpu.VMEM((9, L2 // 2, LANES), F32),
            pltpu.VMEM((L2 // 2, LANES), F32),
            pltpu.VMEM((L2 // 2, LANES), F32),
            pltpu.VMEM((48, LANES), F32),
            pltpu.VMEM((LANES, LANES), BF16),
            pltpu.VMEM((2 * LANES, 2 * LANES), BF16),
            pltpu.VMEM((PADDED, LANES), F32),
            pltpu.VMEM((48, L2, LANES), F32),
            pltpu.VMEM((48, LANES), F32),
            pltpu.VMEM((9, 4, L2, LANES), F32),
            pltpu.VMEM((9, L2, LANES), F32),
            pltpu.VMEM((9, L2, LANES), F32),
            pltpu.VMEM((9, 4, L2, LANES), F32),
            pltpu.VMEM((9, L2, LANES), F32),
            pltpu.VMEM((9, L2, LANES), F32),
        ]
        + [dma((9,))] * 13,
        compiler_params=pltpu.CompilerParams(
            collective_id=0, has_side_effects=True, vmem_limit_bytes=56 << 20
        ),
    )(t, structure, species.reshape(DEPTH), members.reshape(DEPTH, WINDOW), dtab)
    tau = tau.reshape(L2, DEPTH, L2).transpose(1, 0, 2)
    return tau.reshape(1, 1, 1, DEPTH, L2 * L2), pair.reshape(1, 1, DEPTH, WINDOW)


def solution(mesh):
    placed = (
        P(None, "gx", "gy", "gz", None),
        P(),
        P("gx", "gy", "gz"),
        P("gx", "gy", "gz", None),
        P(),
    )
    return jax.shard_map(
        body,
        mesh=mesh,
        in_specs=placed,
        out_specs=(P(None, "gx", "gy", "gz", None), P("gx", "gy", "gz", None)),
        check_vma=False,
    )
```

profile of v0, /device:TPU:1, one launch (start us, length us, event | category | flops | bytes accessed | tf_op | source)
XLA Modules:
  0.0 46.0 jit_solution(12218507213115050414)
XLA Ops:
  0.6 0.8 %tile.10 = f32[4,32,32]{2,1,0:T(8,128)S(1)} reshape(f32[4,1024]{1,0:T(4,128)} %param.9) | data formatting | bytes 32768 | tf_op jit(solution)/shard_map/tile | solution.py:376
  1.5 0.8 %tile.12.dtab_ref = f32[4,32,128]{2,1,0:T(8,128)} reshape(f32[4,32,4,32]{3,2,1,0:T(4,128)S(1)} %tile.11) | data formatting | bytes 131072 | tf_op jit(solution)/shard_map/tile | solution.py:376
  2.3 0.8 %reshape.29 = f32[4,32,32]{2,1,0:T(8,128)S(1)} reshape(f32[1,1,1,4,1024]{4,3,2,1,0:T(4,128)} %param.5) | data formatting | bytes 32768 | tf_op jit(solution)/shard_map/reshape | solution.py:375
  3.1 0.7 %reshape.30.t_ref = f32[32,128]{1,0:T(8,128)} reshape(f32[32,4,32]{2,1,0:T(4,128)S(1)} %bitcast.7) | data formatting | bytes 32768 | tf_op jit(solution)/shard_map/reshape | solution.py:375
  3.8 39.4 %shard_map.68 = (f32[32,128]{1,0:T(8,128)}, f32[4,45]{1,0:T(4,128)}) custom-call(f32[32,128]{1,0:T(8,128)} %reshape.30.t_ref, f32[1,1440,1440]{2,1,0:T(8,128)} %s_hbm.1, s32[4]{0:T(128)} %bitcast.11, s32[4,45]{1,0:T(4,128)} %bitcast.9, f32[4,32,128]{2,1,0:T(8,128)} %tile.12.dtab_ref), custom_call_target="tpu_custom_call" | custom-call | tf_op jit(solution)/shard_map/pallas_call | solution.py:379
  43.2 0.8 %reshape.33 = f32[32,4,32]{2,1,0:T(4,128)S(1)} reshape(f32[32,128]{1,0:T(8,128)} %get-tuple-element.4) | data formatting | bytes 32768 | tf_op jit(solution)/shard_map/reshape | solution.py:422
  44.1 0.7 %reshape.34 = f32[1,1,1,4,1024]{4,3,2,1,0:T(4,128)} reshape(f32[4,32,32]{2,1,0:T(8,128)S(1)} %copy.8) | data formatting | bytes 32768 | tf_op jit(solution)/shard_map/reshape | solution.py:423
  44.8 1.3 %copy.12 = f32[1,1,4,45]{3,2,1,0:T(4,128)} copy(f32[1,1,4,45]{3,2,1,0:T(4,128)} %bitcast.10) | data formatting | bytes 1440
  (3 shorter events, 0.1 us)
where the time goes:
time: 46.4 us; the launch traced here: 46 us
  Pallas kernels  39.4 us (85%)
  local copies, waits for them, and re-layouts  5.96 us (13%)
  between operations  0.67 us (1%)
    pallas_call x1, Pallas kernels, body(): pl.pallas_call(kernel, out_shape=(jax.ShapeDtypeStruct((L2, LANES), F32),...  39.4 us
    another operation x3, local copies, waits for them, and re-layouts, body(): dtab = jnp.tile(delta_table.reshape(SPECIES, L2, L2), (1, 1, DEPTH))  1.63 us
    reshape x3, local copies, waits for them, and re-layouts, body(): t = t_matrix.reshape(DEPTH, L2, L2).transpose(1, 0, 2).reshape(L2, LANES)  1.55 us
    unnamed x1, local copies, waits for them, and re-layouts  1.26 us

commit v1 on v0

--- a/solution.py
+++ b/solution.py
@@ -30,12 +30,23 @@
     return jnp.dot(a, b, preferred_element_type=F32)
 
 
+def turned4(p):
+    q = jnp.concatenate([p, p], axis=0)
+    row = lax.broadcasted_iota(jnp.int32, (8, LANES), 0)
+    block = lax.broadcasted_iota(jnp.int32, (8, LANES), 1) // L2
+    out = q
+    for d in range(1, 4):
+        moved = pltpu.roll(pltpu.roll(q, L2 * d, 1), 8 - d, 0)
+        out = jnp.where((block - row + 8) % 4 == d, moved, out)
+    return out[:4]
+
+
 def kernel(
     t_ref,
     s_hbm,
     species_ref,
     members_ref,
-    dtab_ref,
+    table_ref,
     tau_ref,
     pair_ref,
     sf,
@@ -51,6 +62,8 @@
     mask,
     blocks,
     dbd,
+    tc,
+    image1,
     rnat,
     rb,
     prow,
@@ -107,7 +120,9 @@
 
     lane = lax.broadcasted_iota(jnp.int32, (L2, LANES), 1)
     lane16 = lax.broadcasted_iota(jnp.int32, (L2 // 2, LANES), 1)
-    t = t_ref[...]
+    for k in range(8):
+        tc[4 * k : 4 * k + 4, :] = turned4(t_ref[:, k * LANES : (k + 1) * LANES])
+    t = tc[...]
     top, low = t[: L2 // 2], t[L2 // 2 :]
     pack_u[...] = jnp.where(lane16 < 64, pltpu.roll(top, 64, 1), low)
     pack_d[...] = jnp.where(lane16 < 64, top, pltpu.roll(low, 64, 1))
@@ -125,10 +140,12 @@
             device_id_type=MESH,
         )
 
-    def halo(plane):
+    def halo(plane, aside=True):
         dx, dy = plane // 3 - 1, lax.rem(plane, 3) - 1
         slot = 8 - plane
-        c = remote(t_ref, halo_c.at[slot], hc_send.at[plane], hc_recv.at[slot], peer(dx, dy, 0))
+        c = None
+        if aside:
+            c = remote(tc, halo_c.at[slot], hc_send.at[plane], hc_recv.at[slot], peer(dx, dy, 0))
         u = remote(pack_u, halo_l.at[slot], hl_send.at[plane], hl_recv.at[slot], peer(dx, dy, 1))
         d = remote(pack_d, halo_r.at[slot], hr_send.at[plane], hr_recv.at[slot], peer(dx, dy, -1))
         return c, u, d
@@ -157,11 +174,18 @@
     bc = lax.broadcasted_iota(jnp.int32, (LANES, LANES), 1)
     blocks[...] = jnp.where(br // L2 == bc // L2, 1.0, 0.0).astype(BF16)
 
+    deltas = jnp.concatenate(
+        [turned4(table_ref[:, k * LANES : (k + 1) * LANES]) for k in range(8)], axis=0
+    )
+    code = jnp.zeros((L2, LANES), jnp.int32)
     for s in range(DEPTH):
-        own = dtab_ref[0]
-        for k in range(1, SPECIES):
-            own = jnp.where(species_ref[s] == k, dtab_ref[k], own)
-        dh, dl = split(jnp.where(lane // L2 == s, own, 0.0))
+        code = jnp.where(lane // L2 == s, s + 4 - species_ref[s], code)
+    code = code % 4
+    chosen = deltas
+    for m in range(1, 4):
+        chosen = jnp.where(code == m, pltpu.roll(deltas, L2 * m, 1), chosen)
+    for s in range(DEPTH):
+        dh, dl = split(jnp.where(lane // L2 == s, chosen, 0.0))
         rows = slice(s * L2, (s + 1) * L2)
         down = slice(LANES + s * L2, LANES + (s + 1) * L2)
         dbd[rows, :LANES] = dh
@@ -177,22 +201,24 @@
     sh[:, ROWS:] = jnp.zeros((ROWS, PADDED - ROWS), BF16)
     sl[:, ROWS:] = jnp.zeros((ROWS, PADDED - ROWS), BF16)
 
-    @pl.loop(0, 9)
+    @pl.loop(0, 3)
     def _(i):
-        rows_copy(i).wait()
-        rows = pl.ds(pl.multiple_of(i * 160, 160), 160)
+        for j in range(3):
+            rows_copy(3 * i + j).wait()
+        rows = pl.ds(pl.multiple_of(i * CHUNK, CHUNK), CHUNK)
         high, rest = split(sf[rows, :])
         sh[rows, :ROWS] = high
         sl[rows, :ROWS] = rest
 
-    @pl.loop(0, 9)
-    def _(plane):
-        c, u, d = halo(8 - plane)
-
-        @pl.when(plane != 4)
-        def _():
+    wide = w[0, 512:768, :]
+    a = dot(sh[:, 512:768], wide)
+    b = dot(sl[:, 512:768], wide[:, :LANES])
+    image1[...] = a[:, :LANES] + (a[:, LANES:] + b)
+
+    def windows_of(plane):
+        c, u, d = halo(8 - plane, plane != 4)
+        if plane != 4:
             c.wait_recv()
-
         u.wait_recv()
         d.wait_recv()
         centre = halo_c[plane]
@@ -208,51 +234,54 @@
         ]
         for k in range(5):
             cell = plane * 5 + k
-            th, tl = split(windows[k] * mask[pl.ds(cell, 1), :])
+            th, tl = split(windows[k] * mask[cell : cell + 1, :])
             tw[cell, :L2] = th
             tw[cell, L2:] = tl
 
-    def chunk(g, now, later, first=False, last=False):
-        rows = pl.ds(pl.multiple_of(g * CHUNK, CHUNK), CHUNK)
-        if first:
-            wide = w[0, 512:768, :]
-            a = dot(sh[rows, 512:768], wide)
-            b = dot(sl[rows, 512:768], wide[:, :LANES])
-        else:
-            wide = w[now]
-            a = dot(sh[rows, :], wide)
-            b = dot(sl[rows, :], wide[:, :LANES])
-        image = a[:, :LANES] + (a[:, LANES:] + b)
+    def blocks_times(image, cell, on):
+        ih, il = split(image)
+        wbd = jnp.concatenate(
+            [
+                jnp.concatenate([ih] * DEPTH, axis=0) * on,
+                jnp.concatenate([il] * DEPTH, axis=0) * on,
+            ],
+            axis=1,
+        )
+        res = dot(tw[cell], wbd)
+        x = res[:L2, :LANES] + (res[:L2, LANES:] + res[L2:, :LANES])
+        return x + tc[...] if cell == CENTRE else x
+
+    def both(x):
+        return jnp.concatenate(split(x), axis=1)
+
+    def images(rows, now):
+        wide = w[now]
+        a = dot(sh[rows, :], wide)
+        b = dot(sl[rows, :], wide[:, :LANES])
+        return a[:, :LANES] + (a[:, LANES:] + b)
+
+    def sweep(now, later):
+        image = images(slice(0, ROWS), now)
+        on = blocks[...]
+        for cell in range(WINDOW):
+            rows = slice(cell * L2, (cell + 1) * L2)
+            w[later, rows, :] = both(blocks_times(image[rows], cell, on))
+
+    def last_sweep(now, g):
+        start = g * CHUNK
+        image = images(slice(start, start + CHUNK), now)
         on = blocks[...]
         columns = []
         for i in range(CELLS):
-            ih, il = split(image[i * L2 : (i + 1) * L2])
-            wbd = jnp.concatenate(
-                [
-                    jnp.concatenate([ih] * DEPTH, axis=0) * on,
-                    jnp.concatenate([il] * DEPTH, axis=0) * on,
-                ],
-                axis=1,
-            )
-            res = dot(tw[g * CELLS + i], wbd)
-            x = res[:L2, :LANES] + (res[:L2, LANES:] + res[L2:, :LANES])
-            if i == CELLS // 2:
-                x = x + t_ref[...] * jnp.where(g == 1, 1.0, 0.0).astype(F32)
-                if last:
-
-                    @pl.when(g == 1)
-                    def _():
-                        tau_ref[...] = x
-
-            xh, xl = split(x)
-            columns.append(jnp.concatenate([xh, xl], axis=1))
-        columns = jnp.concatenate(columns, axis=0)
-        if not last:
-            w[later, rows, :] = columns
-            return
-        r2 = dot(columns, dbd[...])
+            cell = g * CELLS + i
+            x = blocks_times(image[i * L2 : (i + 1) * L2], cell, on)
+            if cell == CENTRE:
+                for k in range(8):
+                    tau_ref[:, k * LANES : (k + 1) * LANES] = turned4(x[4 * k : 4 * k + 4])
+            columns.append(both(x))
+        r2 = dot(jnp.concatenate(columns, axis=0), dbd[...])
         r = r2[:, :LANES] + r2[:, LANES:]
-        rnat[rows, :] = r
+        rnat[start : start + CHUNK, :] = r
         for j in range(3):
             turned = []
             for k in range(5):
@@ -260,66 +289,59 @@
                 block = r[at : at + L2]
                 turned.append(pltpu.roll(block, (L2 * (k - 2)) % LANES, 1) if k != 2 else block)
             plane = g * 3 + j
-            kept = [
-                turned[2],
-                turned[3],
-                turned[1],
-                jnp.where(lane >= 64, turned[4], turned[0]),
-            ]
+            target = mrecv if plane == 4 else msend
             usend[plane] = jnp.where(lane < 64, turned[4], pltpu.roll(turned[3], 64, 1))
             dsend[plane] = jnp.where(lane >= 64, turned[0], pltpu.roll(turned[1], 64, 1))
-            c, u, d = pairs(plane)
+            target[plane, 0] = turned[2]
+            target[plane, 1] = turned[3]
+            target[plane, 2] = turned[1]
+            target[plane, 3] = jnp.where(lane >= 64, turned[4], turned[0])
+            c, u, d = pairs(plane, plane != 4)
+            if plane != 4:
+                c.start()
             u.start()
             d.start()
 
-            def away():
-                for n in range(4):
-                    msend[plane, n] = kept[n]
-                c.start()
-
-            if j == 1:
-                pl.when(g != 1)(away)
-
-                @pl.when(g == 1)
-                def _():
-                    for n in range(4):
-                        mrecv[4, n] = kept[n]
-            else:
-                away()
-
-    def pairs(plane):
+    def pairs(plane, aside=True):
         dx, dy = plane // 3 - 1, lax.rem(plane, 3) - 1
-        c = remote(msend.at[plane], mrecv.at[plane], m_send.at[plane], m_recv.at[plane], peer(dx, dy, 0))
+        c = None
+        if aside:
+            c = remote(msend.at[plane], mrecv.at[plane], m_send.at[plane], m_recv.at[plane], peer(dx, dy, 0))
         u = remote(usend.at[plane], urecv.at[plane], u_send.at[plane], u_recv.at[plane], peer(dx, dy, 1))
         d = remote(dsend.at[plane], drecv.at[plane], d_send.at[plane], d_recv.at[plane], peer(dx, dy, -1))
         return c, u, d
 
-    @pl.loop(0, 3)
-    def _(g):
-        chunk(g, 0, 1, first=True)
-
-    @pl.loop(0, (ITERS - 2) * 3)
+    for g in (1, 0, 2):
+        for j in range(3):
+            windows_of(3 * g + j)
+        on = blocks[...]
+        for cell in range(g * CELLS, (g + 1) * CELLS):
+            rows = slice(cell * L2, (cell + 1) * L2)
+            w[1, rows, :] = both(blocks_times(image1[rows, :], cell, on))
+
+    @pl.loop(1, ITERS - 1)
     def _(n):
-        now = lax.rem(n // 3 + 1, 2)
-        chunk(lax.rem(n, 3), now, 1 - now)
+        now = lax.rem(n, 2)
+        sweep(now, 1 - now)
+
+    for g in (0, 2, 1):
+        last_sweep((ITERS - 1) % 2, g)
+
+    rnat[ROWS:, :] = jnp.zeros((PADDED - ROWS, LANES), F32)
 
     @pl.loop(0, 3)
     def _(n):
-        chunk(lax.rem(2 * n, 3), (ITERS - 1) % 2, 0, last=True)
-
-    rnat[ROWS:, :] = jnp.zeros((PADDED - ROWS, LANES), F32)
-
-    @pl.loop(0, 12)
-    def _(i):
-        turned = rnat[pl.ds(pl.multiple_of(i * LANES, LANES), LANES), :].T
-        for j in range(4):
-            out = None
-            for s in range(DEPTH):
-                part = turned[s * L2 : (s + 1) * L2]
-                shift = (L2 * (s - j)) % LANES
-                part = pltpu.roll(part, shift, 1) if shift else part
-                out = part if out is None else jnp.where(lane // L2 == s, part, out)
-            rb[i * 4 + j] = out
+        for m in range(4):
+            i = 4 * n + m
+            turned = rnat[pl.ds(pl.multiple_of(i * LANES, LANES), LANES), :].T
+            for j in range(4):
+                out = None
+                for s in range(DEPTH):
+                    part = turned[s * L2 : (s + 1) * L2]
+                    shift = (L2 * (s - j)) % LANES
+                    part = pltpu.roll(part, shift, 1) if shift else part
+                    out = part if out is None else jnp.where(lane // L2 == s, part, out)
+                rb[i * 4 + j] = out
 
     @pl.loop(0, 9)
     def _(n):
@@ -348,9 +370,9 @@
     prow[WINDOW:, :] = jnp.zeros((48 - WINDOW, LANES), F32)
     sr = lax.broadcasted_iota(jnp.int32, (8, LANES), 0)
     sc = lax.broadcasted_iota(jnp.int32, (8, LANES), 1)
-    chosen = jnp.where(sc // L2 == sr, 1.0, 0.0).astype(F32)
+    summed = jnp.where(sc // L2 == sr, 1.0, 0.0).astype(F32)
     sums = lax.dot_general(
-        chosen,
+        summed,
         prow[...],
         (((1,), (1,)), ((), ())),
         precision=lax.Precision.HIGHEST,
@@ -372,19 +394,17 @@
 
 
 def body(t_matrix, structure, species, members, delta_table):
-    t = t_matrix.reshape(DEPTH, L2, L2).transpose(1, 0, 2).reshape(L2, LANES)
-    dtab = jnp.tile(delta_table.reshape(SPECIES, L2, L2), (1, 1, DEPTH))
     vmem = pl.BlockSpec(memory_space=pltpu.VMEM)
     dma = pltpu.SemaphoreType.DMA
     tau, pair = pl.pallas_call(
         kernel,
         out_shape=(
-            jax.ShapeDtypeStruct((L2, LANES), F32),
+            jax.ShapeDtypeStruct((DEPTH, L2 * L2), F32),
             jax.ShapeDtypeStruct((DEPTH, WINDOW), F32),
         ),
         in_specs=[
             vmem,
-            pl.BlockSpec(memory_space=pl.ANY),
+            pl.BlockSpec(memory_space=pltpu.HBM),
             pl.BlockSpec(memory_space=pltpu.SMEM),
             vmem,
             vmem,
@@ -404,6 +424,8 @@
             pltpu.VMEM((48, LANES), F32),
             pltpu.VMEM((LANES, LANES), BF16),
             pltpu.VMEM((2 * LANES, 2 * LANES), BF16),
+            pltpu.VMEM((L2, LANES), F32),
+            pltpu.VMEM((ROWS, LANES), F32),
             pltpu.VMEM((PADDED, LANES), F32),
             pltpu.VMEM((48, L2, LANES), F32),
             pltpu.VMEM((48, LANES), F32),
@@ -416,10 +438,15 @@
         ]
         + [dma((9,))] * 13,
         compiler_params=pltpu.CompilerParams(
-            collective_id=0, has_side_effects=True, vmem_limit_bytes=56 << 20
+            collective_id=0, has_side_effects=True, vmem_limit_bytes=57 << 20
         ),
-    )(t, structure, species.reshape(DEPTH), members.reshape(DEPTH, WINDOW), dtab)
-    tau = tau.reshape(L2, DEPTH, L2).transpose(1, 0, 2)
+    )(
+        t_matrix.reshape(DEPTH, L2 * L2),
+        structure,
+        species.reshape(DEPTH),
+        members.reshape(DEPTH, WINDOW),
+        delta_table,
+    )
     return tau.reshape(1, 1, 1, DEPTH, L2 * L2), pair.reshape(1, 1, DEPTH, WINDOW)
 
 

time: 46.4 us -> 40.9 us (0.88)
  local copies, waits for them, and re-layouts: 5.96 us -> 2.55 us
  Pallas kernels: 39.4 us -> 37.4 us
    reshape x5 -> x0, local copies, waits for them, and re-layouts: 3.06 us -> none  [the longest x3 1.55 us: body(): t = t_matrix.reshape(DEPTH, L2, L2).transpose(1, 0, 2).reshape(L2, LANES)]
    pallas_call x1, Pallas kernels: 39.4 us -> 37.4 us  [body(): pl.pallas_call(kernel, out_shape=(jax.ShapeDtypeStruct((DEPTH, L2 * L2),...]
    another operation x3 -> x0, local copies, waits for them, and re-layouts: 1.63 us -> none  [body(): dtab = jnp.tile(delta_table.reshape(SPECIES, L2, L2), (1, 1, DEPTH))]
    unnamed x1 -> x2, local copies, waits for them, and re-layouts: 1.26 us -> 2.55 us
where the time goes in v1:
time: 40.9 us; the launch traced here: 40.6 us
  Pallas kernels  37.4 us (91%)
  local copies, waits for them, and re-layouts  2.55 us (6%)
  between operations  0.64 us (2%)
    pallas_call x1, Pallas kernels, body(): pl.pallas_call(kernel, out_shape=(jax.ShapeDtypeStruct((DEPTH, L2 * L2),...  37.4 us
    unnamed x2, local copies, waits for them, and re-layouts  2.55 us

profile of v1, /device:TPU:1, one launch (start us, length us, event | category | flops | bytes accessed | tf_op | source)
XLA Modules:
  0.0 40.6 jit_solution(15411162750226556182)
XLA Ops:
  0.6 37.4 %shard_map.68 = (f32[4,1024]{1,0:T(4,128)}, f32[4,45]{1,0:T(4,128)}) custom-call(f32[4,1024]{1,0:T(4,128)} %bitcast.5, f32[1,1440,1440]{2,1,0:T(8,128)} %s_hbm.1, s32[4]{0:T(128)} %bitcast.9, s32[4,45]{1,0:T(4,128)} %bitcast.7, f32[4,1024]{1,0:T(4,128)} %table_ref.1), custom_call_target="tpu_custom_call" | custom-call | tf_op jit(solution)/shard_map/pallas_call | solution.py:399
  38.0 1.3 %copy.9 = f32[1,1,1,4,1024]{4,3,2,1,0:T(4,128)} copy(f32[1,1,1,4,1024]{4,3,2,1,0:T(4,128)} %bitcast.6) | data formatting | bytes 32768
  39.3 1.2 %copy.10 = f32[1,1,4,45]{3,2,1,0:T(4,128)} copy(f32[1,1,4,45]{3,2,1,0:T(4,128)} %bitcast.8) | data formatting | bytes 1440

commit v2 on v1

--- a/solution.py
+++ b/solution.py
@@ -19,6 +19,15 @@
 F32 = jnp.float32
 BF16 = jnp.bfloat16
 MESH = pl.DeviceIdType.MESH
+ORDER = (0, 8, 2, 6, 3, 5, 1, 7, 4)
+OFFSETS = sorted(
+    [(x, y, z) for x in (-1, 0, 1) for y in (-1, 0, 1) for z in (-1, 0, 1) if x or y or z],
+    key=lambda o: -(abs(o[0]) + abs(o[1]) + abs(o[2])),
+)
+
+
+def cell_at(position):
+    return ORDER[position // 5] * 5 + position % 5
 
 
 def split(x):
@@ -90,35 +99,29 @@
     gx, gy, gz = lax.axis_index("gx"), lax.axis_index("gy"), lax.axis_index("gz")
     nx, ny, nz = lax.axis_size("gx"), lax.axis_size("gy"), lax.axis_size("gz")
 
+    xs = (lax.rem(gx + nx - 1, nx), gx, lax.rem(gx + 1, nx))
+    ys = (lax.rem(gy + ny - 1, ny), gy, lax.rem(gy + 1, ny))
+    zs = (lax.rem(gz + nz - 1, nz), gz, lax.rem(gz + 1, nz))
+
     def peer(dx, dy, dz):
-        return (
-            lax.rem(gx + dx + nx, nx),
-            lax.rem(gy + dy + ny, ny),
-            lax.rem(gz + dz + nz, nz),
+        return (xs[dx + 1], ys[dy + 1], zs[dz + 1])
+
+    barrier = pltpu.get_barrier_semaphore()
+    for offset in OFFSETS:
+        pl.semaphore_signal(barrier, inc=1, device_id=peer(*offset), device_id_type=MESH)
+
+    def rows_copy(i):
+        return pltpu.make_async_copy(
+            s_hbm.at[0, pl.ds(ORDER[i] * 160, 160), :],
+            sf.at[pl.ds(i * 160, 160), :],
+            s_sem.at[i],
         )
 
-    def rows_copy(i):
-        rows = pl.ds(pl.multiple_of(i * 160, 160), 160)
-        return pltpu.make_async_copy(s_hbm.at[0, rows, :], sf.at[rows, :], s_sem.at[i])
-
-    @pl.loop(0, 9)
-    def _(i):
+    for i in range(9):
         rows_copy(i).start()
 
-    barrier = pltpu.get_barrier_semaphore()
-
-    @pl.loop(0, 27)
-    def _(n):
-        @pl.when(n != 13)
-        def _():
-            pl.semaphore_signal(
-                barrier,
-                inc=1,
-                device_id=peer(n // 9 - 1, lax.rem(n // 3, 3) - 1, lax.rem(n, 3) - 1),
-                device_id_type=MESH,
-            )
-
     lane = lax.broadcasted_iota(jnp.int32, (L2, LANES), 1)
+    lane8 = lax.broadcasted_iota(jnp.int32, (8, LANES), 1)
     lane16 = lax.broadcasted_iota(jnp.int32, (L2 // 2, LANES), 1)
     for k in range(8):
         tc[4 * k : 4 * k + 4, :] = turned4(t_ref[:, k * LANES : (k + 1) * LANES])
@@ -140,26 +143,18 @@
             device_id_type=MESH,
         )
 
-    def halo(plane, aside=True):
-        dx, dy = plane // 3 - 1, lax.rem(plane, 3) - 1
+    def halo(offset):
+        dx, dy, dz = offset
+        plane = (dx + 1) * 3 + dy + 1
         slot = 8 - plane
-        c = None
-        if aside:
-            c = remote(tc, halo_c.at[slot], hc_send.at[plane], hc_recv.at[slot], peer(dx, dy, 0))
-        u = remote(pack_u, halo_l.at[slot], hl_send.at[plane], hl_recv.at[slot], peer(dx, dy, 1))
-        d = remote(pack_d, halo_r.at[slot], hr_send.at[plane], hr_recv.at[slot], peer(dx, dy, -1))
-        return c, u, d
-
-    @pl.loop(0, 9)
-    def _(plane):
-        c, u, d = halo(plane)
-
-        @pl.when(plane != 4)
-        def _():
-            c.start()
-
-        u.start()
-        d.start()
+        source = (pack_d, tc, pack_u)[dz + 1]
+        target = (halo_r, halo_c, halo_l)[dz + 1]
+        send = (hr_send, hc_send, hl_send)[dz + 1]
+        recv = (hr_recv, hc_recv, hl_recv)[dz + 1]
+        return remote(source, target.at[slot], send.at[plane], recv.at[slot], peer(*offset))
+
+    for offset in OFFSETS:
+        halo(offset).start()
 
     cells = lax.broadcasted_iota(jnp.int32, (48, WINDOW), 0)
     lane48 = lax.broadcasted_iota(jnp.int32, (48, LANES), 1)
@@ -201,11 +196,10 @@
     sh[:, ROWS:] = jnp.zeros((ROWS, PADDED - ROWS), BF16)
     sl[:, ROWS:] = jnp.zeros((ROWS, PADDED - ROWS), BF16)
 
-    @pl.loop(0, 3)
-    def _(i):
+    for i in range(3):
         for j in range(3):
             rows_copy(3 * i + j).wait()
-        rows = pl.ds(pl.multiple_of(i * CHUNK, CHUNK), CHUNK)
+        rows = pl.ds(i * CHUNK, CHUNK)
         high, rest = split(sf[rows, :])
         sh[rows, :ROWS] = high
         sl[rows, :ROWS] = rest
@@ -216,11 +210,10 @@
     image1[...] = a[:, :LANES] + (a[:, LANES:] + b)
 
     def windows_of(plane):
-        c, u, d = halo(8 - plane, plane != 4)
-        if plane != 4:
-            c.wait_recv()
-        u.wait_recv()
-        d.wait_recv()
+        dx, dy = plane // 3 - 1, plane % 3 - 1
+        for dz in (-1, 0, 1):
+            if (dx, dy, dz) != (0, 0, 0):
+                halo((-dx, -dy, -dz)).wait_recv()
         centre = halo_c[plane]
         up, down = halo_l[plane], halo_r[plane]
         left = jnp.concatenate([pltpu.roll(up, 64, 1), up], axis=0)
@@ -263,17 +256,19 @@
     def sweep(now, later):
         image = images(slice(0, ROWS), now)
         on = blocks[...]
-        for cell in range(WINDOW):
-            rows = slice(cell * L2, (cell + 1) * L2)
-            w[later, rows, :] = both(blocks_times(image[rows], cell, on))
-
-    def last_sweep(now, g):
-        start = g * CHUNK
-        image = images(slice(start, start + CHUNK), now)
+        for i in range(WINDOW):
+            cell = cell_at(i)
+            x = blocks_times(image[i * L2 : (i + 1) * L2], cell, on)
+            w[later, cell * L2 : (cell + 1) * L2, :] = both(x)
+
+    def last_sweep(now, planes):
+        start = planes[0] * 160
+        size = len(planes) * 160
+        image = images(slice(start, start + size), now)
         on = blocks[...]
         columns = []
-        for i in range(CELLS):
-            cell = g * CELLS + i
+        for i in range(size // L2):
+            cell = cell_at(planes[0] * 5 + i)
             x = blocks_times(image[i * L2 : (i + 1) * L2], cell, on)
             if cell == CENTRE:
                 for k in range(8):
@@ -281,51 +276,73 @@
             columns.append(both(x))
         r2 = dot(jnp.concatenate(columns, axis=0), dbd[...])
         r = r2[:, :LANES] + r2[:, LANES:]
-        rnat[start : start + CHUNK, :] = r
-        for j in range(3):
+        for j, position in enumerate(planes):
+            plane = ORDER[position]
+            rnat[plane * 160 : (plane + 1) * 160, :] = r[j * 160 : (j + 1) * 160]
             turned = []
             for k in range(5):
-                at = (j * 5 + k) * L2
+                at = j * 160 + k * L2
                 block = r[at : at + L2]
                 turned.append(pltpu.roll(block, (L2 * (k - 2)) % LANES, 1) if k != 2 else block)
-            plane = g * 3 + j
+            usend[plane, :16] = jnp.where(
+                lane16 < 64, turned[4][:16], pltpu.roll(turned[4][16:], 64, 1)
+            )
+            usend[plane, 16:] = quarter(turned[3], 0)
+            dsend[plane, :16] = jnp.where(
+                lane16 >= 64, turned[0][:16], pltpu.roll(turned[0][16:], 64, 1)
+            )
+            dsend[plane, 16:] = quarter(turned[1], 3)
             target = mrecv if plane == 4 else msend
-            usend[plane] = jnp.where(lane < 64, turned[4], pltpu.roll(turned[3], 64, 1))
-            dsend[plane] = jnp.where(lane >= 64, turned[0], pltpu.roll(turned[1], 64, 1))
-            target[plane, 0] = turned[2]
-            target[plane, 1] = turned[3]
-            target[plane, 2] = turned[1]
-            target[plane, 3] = jnp.where(lane >= 64, turned[4], turned[0])
-            c, u, d = pairs(plane, plane != 4)
-            if plane != 4:
-                c.start()
-            u.start()
-            d.start()
-
-    def pairs(plane, aside=True):
-        dx, dy = plane // 3 - 1, lax.rem(plane, 3) - 1
-        c = None
-        if aside:
-            c = remote(msend.at[plane], mrecv.at[plane], m_send.at[plane], m_recv.at[plane], peer(dx, dy, 0))
-        u = remote(usend.at[plane], urecv.at[plane], u_send.at[plane], u_recv.at[plane], peer(dx, dy, 1))
-        d = remote(dsend.at[plane], drecv.at[plane], d_send.at[plane], d_recv.at[plane], peer(dx, dy, -1))
-        return c, u, d
-
-    for g in (1, 0, 2):
-        for j in range(3):
-            windows_of(3 * g + j)
+            target[plane, :32] = turned[2]
+            target[plane, 32:64] = jnp.where(lane >= 64, turned[4], turned[0])
+            target[plane, 64:96] = jnp.where(lane < 32, turned[1], turned[3])
+            target[plane, 96:] = jnp.where(
+                (lane16 >= 32) & (lane16 < 96), turned[1][:16], pltpu.roll(turned[1][16:], 64, 1)
+            )
+            for dz in (-1, 1, 0):
+                if plane != 4 or dz:
+                    pairs(plane, dz).start()
+
+    def quarter(x, first):
+        out = x[:8]
+        for m in range(1, 4):
+            moved = pltpu.roll(x[8 * m : 8 * m + 8], L2 * m, 1)
+            out = jnp.where(lane8 // L2 == (first + m) % 4, moved, out)
+        return out
+
+    def unquarter(q):
+        parts = [q] + [pltpu.roll(q, LANES - L2 * m, 1) for m in range(1, 4)]
+        return jnp.concatenate(parts, axis=0)
+
+    def unhalf(h):
+        return jnp.concatenate([h, pltpu.roll(h, 64, 1)], axis=0)
+
+    def pairs(plane, dz):
+        dx, dy = plane // 3 - 1, plane % 3 - 1
+        source = (dsend, msend, usend)[dz + 1]
+        target = (drecv, mrecv, urecv)[dz + 1]
+        send = (d_send, m_send, u_send)[dz + 1]
+        recv = (d_recv, m_recv, u_recv)[dz + 1]
+        return remote(
+            source.at[plane], target.at[plane], send.at[plane], recv.at[plane], peer(dx, dy, dz)
+        )
+
+    for first, past in ((4, 9), (0, 4)):
+        for position in range(past - 1, first - 1, -1):
+            windows_of(ORDER[position])
         on = blocks[...]
-        for cell in range(g * CELLS, (g + 1) * CELLS):
-            rows = slice(cell * L2, (cell + 1) * L2)
-            w[1, rows, :] = both(blocks_times(image1[rows, :], cell, on))
+        for i in range(first * 5, past * 5):
+            cell = cell_at(i)
+            x = blocks_times(image1[i * L2 : (i + 1) * L2, :], cell, on)
+            w[1, cell * L2 : (cell + 1) * L2, :] = both(x)
 
     @pl.loop(1, ITERS - 1)
     def _(n):
         now = lax.rem(n, 2)
         sweep(now, 1 - now)
 
-    for g in (0, 2, 1):
-        last_sweep((ITERS - 1) % 2, g)
+    for planes in ((0, 1), (2, 3), (4, 5), (6, 7), (8,)):
+        last_sweep((ITERS - 1) % 2, planes)
 
     rnat[ROWS:, :] = jnp.zeros((PADDED - ROWS, LANES), F32)
 
@@ -343,29 +360,24 @@
                     out = part if out is None else jnp.where(lane // L2 == s, part, out)
                 rb[i * 4 + j] = out
 
-    @pl.loop(0, 9)
-    def _(n):
-        plane = jnp.where(n == 0, 4, jnp.where(n <= 4, n - 1, n))
-        c, u, d = pairs(plane)
-
-        @pl.when(n != 0)
-        def _():
-            c.wait_recv()
-
-        u.wait_recv()
-        d.wait_recv()
-        up, down = urecv[plane], drecv[plane]
-        split_block = mrecv[plane, 3]
+    for plane in ORDER:
+        for dz in (-1, 0, 1):
+            if plane != 4 or dz:
+                pairs(plane, dz).wait_recv()
+        u2, u1 = unhalf(urecv[plane, :16]), unquarter(urecv[plane, 16:])
+        d2, d1 = unhalf(drecv[plane, :16]), unquarter(drecv[plane, 16:])
+        outer, inner = mrecv[plane, 32:64], mrecv[plane, 64:96]
+        rest = unhalf(mrecv[plane, 96:])
         got = [
-            jnp.where(lane < 64, split_block, down),
-            jnp.where(lane < 96, mrecv[plane, 2], pltpu.roll(down, 64, 1)),
-            mrecv[plane, 0],
-            jnp.where(lane < 32, pltpu.roll(up, 64, 1), mrecv[plane, 1]),
-            jnp.where(lane < 64, up, split_block),
+            jnp.where(lane < 64, outer, d2),
+            jnp.where(lane < 32, inner, jnp.where(lane < 96, rest, d1)),
+            mrecv[plane, :32],
+            jnp.where(lane < 32, u1, inner),
+            jnp.where(lane < 64, u2, outer),
         ]
         for k in range(5):
             cell = WINDOW - 1 - (plane * 5 + k)
-            prow[pl.ds(cell, 1), :] = jnp.sum(got[k] * rb[cell], axis=0, keepdims=True)
+            prow[cell : cell + 1, :] = jnp.sum(got[k] * rb[cell], axis=0, keepdims=True)
 
     prow[WINDOW:, :] = jnp.zeros((48 - WINDOW, LANES), F32)
     sr = lax.broadcasted_iota(jnp.int32, (8, LANES), 0)
@@ -380,17 +392,23 @@
     )
     pair_ref[...] = sums[:DEPTH, :WINDOW]
 
-    @pl.loop(0, 9)
-    def _(plane):
-        for copies in (halo(plane), pairs(plane)):
-            c, u, d = copies
-
-            @pl.when(plane != 4)
-            def _():
-                c.wait_send()
-
-            u.wait_send()
-            d.wait_send()
+    for offset in OFFSETS:
+        halo(offset).wait_send()
+    for plane in ORDER:
+        for dz in (-1, 0, 1):
+            if plane != 4 or dz:
+                pairs(plane, dz).wait_send()
+
+
+def finish(tau_ref, pair_ref, tau_out, pair_out, sem):
+    copies = (
+        pltpu.make_async_copy(tau_ref, tau_out, sem.at[0]),
+        pltpu.make_async_copy(pair_ref, pair_out, sem.at[1]),
+    )
+    for copy in copies:
+        copy.start()
+    for copy in copies:
+        copy.wait()
 
 
 def body(t_matrix, structure, species, members, delta_table):
@@ -429,12 +447,12 @@
             pltpu.VMEM((PADDED, LANES), F32),
             pltpu.VMEM((48, L2, LANES), F32),
             pltpu.VMEM((48, LANES), F32),
-            pltpu.VMEM((9, 4, L2, LANES), F32),
-            pltpu.VMEM((9, L2, LANES), F32),
-            pltpu.VMEM((9, L2, LANES), F32),
-            pltpu.VMEM((9, 4, L2, LANES), F32),
-            pltpu.VMEM((9, L2, LANES), F32),
-            pltpu.VMEM((9, L2, LANES), F32),
+            pltpu.VMEM((9, 112, LANES), F32),
+            pltpu.VMEM((9, 24, LANES), F32),
+            pltpu.VMEM((9, 24, LANES), F32),
+            pltpu.VMEM((9, 112, LANES), F32),
+            pltpu.VMEM((9, 24, LANES), F32),
+            pltpu.VMEM((9, 24, LANES), F32),
         ]
         + [dma((9,))] * 13,
         compiler_params=pltpu.CompilerParams(
@@ -447,6 +465,18 @@
         members.reshape(DEPTH, WINDOW),
         delta_table,
     )
+    anywhere = pl.BlockSpec(memory_space=pl.ANY)
+    tau, pair = pl.pallas_call(
+        finish,
+        out_shape=(
+            jax.ShapeDtypeStruct((DEPTH, L2 * L2), F32),
+            jax.ShapeDtypeStruct((DEPTH, WINDOW), F32),
+        ),
+        in_specs=[anywhere] * 2,
+        out_specs=(anywhere,) * 2,
+        scratch_shapes=[dma((2,))],
+        compiler_params=pltpu.CompilerParams(vmem_limit_bytes=60 << 20),
+    )(tau, pair)
     return tau.reshape(1, 1, 1, DEPTH, L2 * L2), pair.reshape(1, 1, DEPTH, WINDOW)
 
 

time: 40.9 us -> 36.7 us (0.90)
  local copies, waits for them, and re-layouts: 2.55 us -> 0 us
  Pallas kernels: 37.4 us -> 35.9 us
    pallas_call x1, Pallas kernels: 37.4 us -> 34.3 us  [body(): pl.pallas_call(kernel, out_shape=(jax.ShapeDtypeStruct((DEPTH, L2 * L2),...]
    unnamed x2 -> x0, local copies, waits for them, and re-layouts: 2.55 us -> none
    pallas_call x0 -> x1, Pallas kernels: none -> 1.68 us  [body(): pl.pallas_call(finish, out_shape=(jax.ShapeDtypeStruct((DEPTH, L2 * L2),...]
where the time goes in v2:
time: 36.7 us; the launch traced here: 36.6 us
  Pallas kernels  35.9 us (98%)
  between operations  0.64 us (2%)
    pallas_call x1, Pallas kernels, body(): pl.pallas_call(kernel, out_shape=(jax.ShapeDtypeStruct((DEPTH, L2 * L2),...  34.3 us
    pallas_call x1, Pallas kernels, body(): pl.pallas_call(finish, out_shape=(jax.ShapeDtypeStruct((DEPTH, L2 * L2),...  1.68 us

profile of v2, /device:TPU:1, one launch (start us, length us, event | category | flops | bytes accessed | tf_op | source)
XLA Modules:
  0.0 36.6 jit_solution(9622224505331452165)
XLA Ops:
  0.6 34.3 %shard_map.68 = (f32[4,1024]{1,0:T(4,128)}, f32[4,45]{1,0:T(4,128)}) custom-call(f32[4,1024]{1,0:T(4,128)} %bitcast.5, f32[1,1440,1440]{2,1,0:T(8,128)} %s_hbm.1, s32[4]{0:T(128)} %bitcast.7, s32[4,45]{1,0:T(4,128)} %bitcast.6, f32[4,1024]{1,0:T(4,128)} %table_ref.1), custom_call_target="tpu_custom_call" | custom-call | tf_op jit(solution)/shard_map/pallas_call | solution.py:417
  34.9 1.7 %shard_map.69 = (f32[4,1024]{1,0:T(4,128)}, f32[4,45]{1,0:T(4,128)}) custom-call(f32[4,1024]{1,0:T(4,128)} %get-tuple-element.6.tau_ref, f32[4,45]{1,0:T(4,128)} %get-tuple-element.7.pair_ref), custom_call_target="tpu_custom_call" | custom-call | tf_op jit(solution)/shard_map/pallas_call | solution.py:469

commit v3 on v2

--- a/solution.py
+++ b/solution.py
@@ -51,13 +51,17 @@
 
 
 def kernel(
+    t_hbm,
+    s_hbm,
+    species_hbm,
+    members_hbm,
+    table_hbm,
+    tau_ref,
+    pair_ref,
     t_ref,
-    s_hbm,
     species_ref,
     members_ref,
     table_ref,
-    tau_ref,
-    pair_ref,
     sf,
     sh,
     sl,
@@ -82,6 +86,7 @@
     mrecv,
     urecv,
     drecv,
+    in_sem,
     s_sem,
     hc_send,
     hl_send,
@@ -106,6 +111,20 @@
     def peer(dx, dy, dz):
         return (xs[dx + 1], ys[dy + 1], zs[dz + 1])
 
+    inputs = [
+        pltpu.make_async_copy(source, target, in_sem.at[i])
+        for i, (source, target) in enumerate(
+            (
+                (t_hbm, t_ref),
+                (species_hbm, species_ref),
+                (members_hbm, members_ref),
+                (table_hbm, table_ref),
+            )
+        )
+    ]
+    for copy in inputs:
+        copy.start()
+
     barrier = pltpu.get_barrier_semaphore()
     for offset in OFFSETS:
         pl.semaphore_signal(barrier, inc=1, device_id=peer(*offset), device_id_type=MESH)
@@ -123,6 +142,7 @@
     lane = lax.broadcasted_iota(jnp.int32, (L2, LANES), 1)
     lane8 = lax.broadcasted_iota(jnp.int32, (8, LANES), 1)
     lane16 = lax.broadcasted_iota(jnp.int32, (L2 // 2, LANES), 1)
+    inputs[0].wait()
     for k in range(8):
         tc[4 * k : 4 * k + 4, :] = turned4(t_ref[:, k * LANES : (k + 1) * LANES])
     t = tc[...]
@@ -156,6 +176,8 @@
     for offset in OFFSETS:
         halo(offset).start()
 
+    for copy in inputs[1:]:
+        copy.wait()
     cells = lax.broadcasted_iota(jnp.int32, (48, WINDOW), 0)
     lane48 = lax.broadcasted_iota(jnp.int32, (48, LANES), 1)
     member = jnp.zeros((48, LANES), F32)
@@ -327,14 +349,13 @@
             source.at[plane], target.at[plane], send.at[plane], recv.at[plane], peer(dx, dy, dz)
         )
 
-    for first, past in ((4, 9), (0, 4)):
-        for position in range(past - 1, first - 1, -1):
-            windows_of(ORDER[position])
-        on = blocks[...]
-        for i in range(first * 5, past * 5):
-            cell = cell_at(i)
-            x = blocks_times(image1[i * L2 : (i + 1) * L2, :], cell, on)
-            w[1, cell * L2 : (cell + 1) * L2, :] = both(x)
+    for plane in ORDER[::-1]:
+        windows_of(plane)
+    on = blocks[...]
+    for i in range(WINDOW):
+        cell = cell_at(i)
+        x = blocks_times(image1[i * L2 : (i + 1) * L2, :], cell, on)
+        w[1, cell * L2 : (cell + 1) * L2, :] = both(x)
 
     @pl.loop(1, ITERS - 1)
     def _(n):
@@ -420,15 +441,13 @@
             jax.ShapeDtypeStruct((DEPTH, L2 * L2), F32),
             jax.ShapeDtypeStruct((DEPTH, WINDOW), F32),
         ),
-        in_specs=[
-            vmem,
-            pl.BlockSpec(memory_space=pltpu.HBM),
-            pl.BlockSpec(memory_space=pltpu.SMEM),
-            vmem,
-            vmem,
-        ],
+        in_specs=[pl.BlockSpec(memory_space=pltpu.HBM)] * 5,
         out_specs=(vmem, vmem),
         scratch_shapes=[
+            pltpu.VMEM((DEPTH, L2 * L2), F32),
+            pltpu.SMEM((DEPTH,), jnp.int32),
+            pltpu.VMEM((DEPTH, WINDOW), jnp.int32),
+            pltpu.VMEM((SPECIES, L2 * L2), F32),
             pltpu.VMEM((ROWS, ROWS), F32),
             pltpu.VMEM((ROWS, PADDED), BF16),
             pltpu.VMEM((ROWS, PADDED), BF16),
@@ -454,16 +473,22 @@
             pltpu.VMEM((9, 24, LANES), F32),
             pltpu.VMEM((9, 24, LANES), F32),
         ]
+        + [dma((4,))]
         + [dma((9,))] * 13,
         compiler_params=pltpu.CompilerParams(
-            collective_id=0, has_side_effects=True, vmem_limit_bytes=57 << 20
+            collective_id=0, has_side_effects=True, vmem_limit_bytes=50 << 20
         ),
     )(
-        t_matrix.reshape(DEPTH, L2 * L2),
-        structure,
-        species.reshape(DEPTH),
-        members.reshape(DEPTH, WINDOW),
-        delta_table,
+        *(
+            pltpu.with_memory_space_constraint(x, pltpu.HBM)
+            for x in (
+                t_matrix.reshape(DEPTH, L2 * L2),
+                structure,
+                species.reshape(DEPTH),
+                members.reshape(DEPTH, WINDOW),
+                delta_table,
+            )
+        )
     )
     anywhere = pl.BlockSpec(memory_space=pl.ANY)
     tau, pair = pl.pallas_call(
@@ -475,7 +500,7 @@
         in_specs=[anywhere] * 2,
         out_specs=(anywhere,) * 2,
         scratch_shapes=[dma((2,))],
-        compiler_params=pltpu.CompilerParams(vmem_limit_bytes=60 << 20),
+        compiler_params=pltpu.CompilerParams(vmem_limit_bytes=16 << 20),
     )(tau, pair)
     return tau.reshape(1, 1, 1, DEPTH, L2 * L2), pair.reshape(1, 1, DEPTH, WINDOW)
 

time: 36.7 us -> 34.8 us (0.948)
  Pallas kernels: 35.9 us -> 34 us
    pallas_call x1, Pallas kernels: 1.68 us -> 0.63 us  [body(): pl.pallas_call(finish, out_shape=(jax.ShapeDtypeStruct((DEPTH, L2 * L2),...]
    pallas_call x1, Pallas kernels: 34.3 us -> 33.4 us  [body(): pl.pallas_call(kernel, out_shape=(jax.ShapeDtypeStruct((DEPTH, L2 * L2),...]
where the time goes in v3:
time: 34.8 us; the launch traced here: 34.6 us
  Pallas kernels  34 us (98%)
  between operations  0.64 us (2%)
    pallas_call x1, Pallas kernels, body(): pl.pallas_call(kernel, out_shape=(jax.ShapeDtypeStruct((DEPTH, L2 * L2),...  33.4 us

profile of v3, /device:TPU:1, one launch (start us, length us, event | category | flops | bytes accessed | tf_op | source)
XLA Modules:
  0.0 34.6 jit_solution(14791103870472608906)
XLA Ops:
  0.6 33.4 %shard_map.68 = (f32[4,1024]{1,0:T(4,128)S(1)}, f32[4,45]{1,0:T(4,128)S(1)}) custom-call(f32[4,1024]{1,0:T(4,128)} %bitcast.5, f32[1,1440,1440]{2,1,0:T(8,128)} %s_hbm.1, s32[4]{0:T(128)} %bitcast.7, s32[4,45]{1,0:T(4,128)} %bitcast.6, f32[4,1024]{1,0:T(4,128)} %table_hbm.1), custom_call_target="tpu_custom_call" | custom-call | tf_op jit(solution)/shard_map/pallas_call | solution.py:438
  34.0 0.6 %shard_map.69 = (f32[4,1024]{1,0:T(4,128)}, f32[4,45]{1,0:T(4,128)}) custom-call(f32[4,1024]{1,0:T(4,128)S(1)} %get-tuple-element.6.tau_ref, f32[4,45]{1,0:T(4,128)S(1)} %get-tuple-element.7.pair_ref), custom_call_target="tpu_custom_call" | custom-call | tf_op jit(solution)/shard_map/pallas_call | solution.py:494

commit v4 on v3

--- a/solution.py
+++ b/solution.py
@@ -212,6 +212,8 @@
 
     w[:, 512:768, :] = jnp.zeros((2, 256, 2 * LANES), BF16)
     w[:, ROWS:, :] = jnp.zeros((2, PADDED - ROWS, 2 * LANES), BF16)
+    rnat[ROWS:, :] = jnp.zeros((PADDED - ROWS, LANES), F32)
+    prow[WINDOW:, :] = jnp.zeros((48 - WINDOW, LANES), F32)
     th, tl = split(t)
     w[0, CENTRE * L2 : (CENTRE + 1) * L2, :LANES] = th
     w[0, CENTRE * L2 : (CENTRE + 1) * L2, LANES:] = tl
@@ -362,10 +364,9 @@
         now = lax.rem(n, 2)
         sweep(now, 1 - now)
 
-    for planes in ((0, 1), (2, 3), (4, 5), (6, 7), (8,)):
+    for planes in ((0, 1, 2), (3, 4, 5), (6, 7, 8)):
         last_sweep((ITERS - 1) % 2, planes)
 
-    rnat[ROWS:, :] = jnp.zeros((PADDED - ROWS, LANES), F32)
 
     @pl.loop(0, 3)
     def _(n):
@@ -400,7 +401,6 @@
             cell = WINDOW - 1 - (plane * 5 + k)
             prow[cell : cell + 1, :] = jnp.sum(got[k] * rb[cell], axis=0, keepdims=True)
 
-    prow[WINDOW:, :] = jnp.zeros((48 - WINDOW, LANES), F32)
     sr = lax.broadcasted_iota(jnp.int32, (8, LANES), 0)
     sc = lax.broadcasted_iota(jnp.int32, (8, LANES), 1)
     summed = jnp.where(sc // L2 == sr, 1.0, 0.0).astype(F32)

time: 34.8 us -> 34.4 us (0.989)
  Pallas kernels: 34 us -> 33.6 us
    pallas_call x1, Pallas kernels: 33.4 us -> 33 us  [body(): pl.pallas_call(kernel, out_shape=(jax.ShapeDtypeStruct((DEPTH, L2 * L2),...]
where the time goes in v4:
time: 34.4 us; the launch traced here: 34.2 us
  Pallas kernels  33.6 us (98%)
  between operations  0.64 us (2%)
    pallas_call x1, Pallas kernels, body(): pl.pallas_call(kernel, out_shape=(jax.ShapeDtypeStruct((DEPTH, L2 * L2),...  33 us

profile of v4, /device:TPU:1, one launch (start us, length us, event | category | flops | bytes accessed | tf_op | source)
XLA Modules:
  0.0 34.2 jit_solution(1896540912687655155)
XLA Ops:
  0.6 33.0 %shard_map.68 = (f32[4,1024]{1,0:T(4,128)S(1)}, f32[4,45]{1,0:T(4,128)S(1)}) custom-call(f32[4,1024]{1,0:T(4,128)} %bitcast.5, f32[1,1440,1440]{2,1,0:T(8,128)} %s_hbm.1, s32[4]{0:T(128)} %bitcast.7, s32[4,45]{1,0:T(4,128)} %bitcast.6, f32[4,1024]{1,0:T(4,128)} %table_hbm.1), custom_call_target="tpu_custom_call" | custom-call | tf_op jit(solution)/shard_map/pallas_call | solution.py:438
  33.6 0.6 %shard_map.69 = (f32[4,1024]{1,0:T(4,128)}, f32[4,45]{1,0:T(4,128)}) custom-call(f32[4,1024]{1,0:T(4,128)S(1)} %get-tuple-element.6.tau_ref, f32[4,45]{1,0:T(4,128)S(1)} %get-tuple-element.7.pair_ref), custom_call_target="tpu_custom_call" | custom-call | tf_op jit(solution)/shard_map/pallas_call | solution.py:494

commit v5 on v4

--- a/solution.py
+++ b/solution.py
@@ -77,6 +77,7 @@
     dbd,
     tc,
     image1,
+    spread1,
     rnat,
     rb,
     prow,
@@ -255,16 +256,21 @@
             tw[cell, :L2] = th
             tw[cell, L2:] = tl
 
-    def blocks_times(image, cell, on):
+    def spread(image, on):
         ih, il = split(image)
-        wbd = jnp.concatenate(
+        return jnp.concatenate(
             [
                 jnp.concatenate([ih] * DEPTH, axis=0) * on,
                 jnp.concatenate([il] * DEPTH, axis=0) * on,
             ],
             axis=1,
         )
-        res = dot(tw[cell], wbd)
+
+    def blocks_times(image, cell, on):
+        return times(spread(image, on), cell)
+
+    def times(wide, cell):
+        res = dot(tw[cell], wide)
         x = res[:L2, :LANES] + (res[:L2, LANES:] + res[L2:, :LANES])
         return x + tc[...] if cell == CENTRE else x
 
@@ -351,12 +357,14 @@
             source.at[plane], target.at[plane], send.at[plane], recv.at[plane], peer(dx, dy, dz)
         )
 
+    on = blocks[...]
+    for i in range(WINDOW):
+        spread1[i] = spread(image1[i * L2 : (i + 1) * L2, :], on)
     for plane in ORDER[::-1]:
         windows_of(plane)
-    on = blocks[...]
     for i in range(WINDOW):
         cell = cell_at(i)
-        x = blocks_times(image1[i * L2 : (i + 1) * L2, :], cell, on)
+        x = times(spread1[i], cell)
         w[1, cell * L2 : (cell + 1) * L2, :] = both(x)
 
     @pl.loop(1, ITERS - 1)
@@ -366,6 +374,9 @@
 
     for planes in ((0, 1, 2), (3, 4, 5), (6, 7, 8)):
         last_sweep((ITERS - 1) % 2, planes)
+
+    for offset in OFFSETS:
+        halo(offset).wait_send()
 
 
     @pl.loop(0, 3)
@@ -400,6 +411,9 @@
         for k in range(5):
             cell = WINDOW - 1 - (plane * 5 + k)
             prow[cell : cell + 1, :] = jnp.sum(got[k] * rb[cell], axis=0, keepdims=True)
+        for dz in (-1, 0, 1):
+            if plane != 4 or dz:
+                pairs(plane, dz).wait_send()
 
     sr = lax.broadcasted_iota(jnp.int32, (8, LANES), 0)
     sc = lax.broadcasted_iota(jnp.int32, (8, LANES), 1)
@@ -412,13 +426,6 @@
         preferred_element_type=F32,
     )
     pair_ref[...] = sums[:DEPTH, :WINDOW]
-
-    for offset in OFFSETS:
-        halo(offset).wait_send()
-    for plane in ORDER:
-        for dz in (-1, 0, 1):
-            if plane != 4 or dz:
-                pairs(plane, dz).wait_send()
 
 
 def finish(tau_ref, pair_ref, tau_out, pair_out, sem):
@@ -463,6 +470,7 @@
             pltpu.VMEM((2 * LANES, 2 * LANES), BF16),
             pltpu.VMEM((L2, LANES), F32),
             pltpu.VMEM((ROWS, LANES), F32),
+            pltpu.VMEM((WINDOW, LANES, 2 * LANES), BF16),
             pltpu.VMEM((PADDED, LANES), F32),
             pltpu.VMEM((48, L2, LANES), F32),
             pltpu.VMEM((48, LANES), F32),

time: 34.4 us -> 34.4 us (level)
  no operation moved by 1% of the time
where the time goes in v5:
time: 34.4 us; the launch traced here: 34.2 us
  Pallas kernels  33.6 us (98%)
  between operations  0.64 us (2%)
    pallas_call x1, Pallas kernels, body(): pl.pallas_call(kernel, out_shape=(jax.ShapeDtypeStruct((DEPTH, L2 * L2),...  32.9 us

profile of v5, /device:TPU:1, one launch (start us, length us, event | category | flops | bytes accessed | tf_op | source)
XLA Modules:
  0.0 34.2 jit_solution(8458217249482843877)
XLA Ops:
  0.6 32.9 %shard_map.68 = (f32[4,1024]{1,0:T(4,128)S(1)}, f32[4,45]{1,0:T(4,128)S(1)}) custom-call(f32[4,1024]{1,0:T(4,128)} %bitcast.5, f32[1,1440,1440]{2,1,0:T(8,128)} %s_hbm.1, s32[4]{0:T(128)} %bitcast.7, s32[4,45]{1,0:T(4,128)} %bitcast.6, f32[4,1024]{1,0:T(4,128)} %table_hbm.1), custom_call_target="tpu_custom_call" | custom-call | tf_op jit(solution)/shard_map/pallas_call | solution.py:445
  33.6 0.6 %shard_map.69 = (f32[4,1024]{1,0:T(4,128)}, f32[4,45]{1,0:T(4,128)}) custom-call(f32[4,1024]{1,0:T(4,128)S(1)} %get-tuple-element.6.tau_ref, f32[4,45]{1,0:T(4,128)S(1)} %get-tuple-element.7.pair_ref), custom_call_target="tpu_custom_call" | custom-call | tf_op jit(solution)/shard_map/pallas_call | solution.py:502

commit v6 on v5

--- a/solution.py
+++ b/solution.py
@@ -372,7 +372,7 @@
         now = lax.rem(n, 2)
         sweep(now, 1 - now)
 
-    for planes in ((0, 1, 2), (3, 4, 5), (6, 7, 8)):
+    for planes in ((0, 1), (2, 3, 4, 5), (6, 7, 8)):
         last_sweep((ITERS - 1) % 2, planes)
 
     for offset in OFFSETS:

time: 34.4 us -> 34.9 us (1.015)
  Pallas kernels: 33.6 us -> 34.1 us
    pallas_call x1, Pallas kernels: 32.9 us -> 33.5 us  [body(): pl.pallas_call(kernel, out_shape=(jax.ShapeDtypeStruct((DEPTH, L2 * L2),...]
where the time goes in v6:
time: 34.9 us; the launch traced here: 34.8 us
  Pallas kernels  34.1 us (98%)
  between operations  0.64 us (2%)
    pallas_call x1, Pallas kernels, body(): pl.pallas_call(kernel, out_shape=(jax.ShapeDtypeStruct((DEPTH, L2 * L2),...  33.5 us

profile of v6, /device:TPU:1, one launch (start us, length us, event | category | flops | bytes accessed | tf_op | source)
XLA Modules:
  0.0 34.8 jit_solution(3327357407895441964)
XLA Ops:
  0.6 33.5 %shard_map.68 = (f32[4,1024]{1,0:T(4,128)S(1)}, f32[4,45]{1,0:T(4,128)S(1)}) custom-call(f32[4,1024]{1,0:T(4,128)} %bitcast.5, f32[1,1440,1440]{2,1,0:T(8,128)} %s_hbm.1, s32[4]{0:T(128)} %bitcast.7, s32[4,45]{1,0:T(4,128)} %bitcast.6, f32[4,1024]{1,0:T(4,128)} %table_hbm.1), custom_call_target="tpu_custom_call" | custom-call | tf_op jit(solution)/shard_map/pallas_call | solution.py:445
  34.1 0.6 %shard_map.69 = (f32[4,1024]{1,0:T(4,128)}, f32[4,45]{1,0:T(4,128)}) custom-call(f32[4,1024]{1,0:T(4,128)S(1)} %get-tuple-element.6.tau_ref, f32[4,45]{1,0:T(4,128)S(1)} %get-tuple-element.7.pair_ref), custom_call_target="tpu_custom_call" | custom-call | tf_op jit(solution)/shard_map/pallas_call | solution.py:502
